TPU v7x, 32 devices: a whole 2x2x4 slice. The times are simulated.
32 devices in a mesh: freq: 8 (over y, x, core), rcv: 4 (over z).
Axes of the slice: x: 2, y: 2, z: 4, core: 2. Of those that a mesh axis runs over, the one named last changes fastest.
Arguments:
- green_freq: float32 [2, 8, 2304, 2304], P(None, 'freq', 'rcv'), may hold values from -6 to 6
- data_matrix: float32 [2, 8, 2304, 2304], P(None, 'freq', 'rcv'), may hold values from -0.09375 to 0.09375
- shot_panels: float32 [2, 8, 2304, 256], P(None, 'freq', 'rcv'), may hold values from -6 to 6
- wavelet: float32 [2, 8], P(None, 'freq'), may hold values from -1.5 to 1.5
- sources: int32 [256], replicated, may hold values from 0 to 2303, as said below
- support: int32 [8, 2304], replicated, may hold values 0 or 1
- threshold: float32 [1], replicated, may hold values from 3 to 7
Outputs:
- green_next: float32 [2, 8, 2304, 2304], P(None, 'freq', 'rcv')
- residual: float32 [2, 8, 2304, 256], P(None, 'freq', 'rcv')
Inputs may be any that keep to these rules, and one draw needn't show every extreme that they name: `sources`: 256 distinct source positions. `support`: a 0/1 mask over time samples and source positions.
All inputs are finite; a program needn't handle non-finite values.
Results may differ from a plain program's by a relative error of at most 0.00013.
Values sent between devices are 32-bit elements; how exact they have to be, the bound alone decides.
A program may use at most 128 MiB of HBM per device.

v0:
```python
import math
import jax
import jax.numpy as jnp
from jax import lax
from jax.sharding import PartitionSpec as P

HIGHEST = lax.Precision.HIGHEST


def complex_product(left_pair, right_pair, pattern):
    left_real, left_imag = left_pair
    right_real, right_imag = right_pair
    real_part = jnp.einsum(pattern, left_real, right_real, precision=HIGHEST) - jnp.einsum(
        pattern, left_imag, right_imag, precision=HIGHEST
    )
    imag_part = jnp.einsum(pattern, left_real, right_imag, precision=HIGHEST) + jnp.einsum(
        pattern, left_imag, right_real, precision=HIGHEST
    )
    return (real_part, imag_part)


def conj_product(left_pair, right_pair, pattern):
    left_real, left_imag = left_pair
    right_real, right_imag = right_pair
    real_part = jnp.einsum(pattern, left_real, right_real, precision=HIGHEST) + jnp.einsum(
        pattern, left_imag, right_imag, precision=HIGHEST
    )
    imag_part = jnp.einsum(pattern, left_real, right_imag, precision=HIGHEST) - jnp.einsum(
        pattern, left_imag, right_real, precision=HIGHEST
    )
    return (real_part, imag_part)


def shrink_spectra(spectra, keep, shrink_level):
    n_freq = spectra.shape[1]
    grid = jnp.arange(n_freq, dtype=jnp.int32)
    phase = grid[:, None] * grid[None, :] % n_freq
    angle = phase.astype(jnp.float32) * (2.0 * math.pi / n_freq)
    cos_table = jnp.cos(angle)
    sin_table = jnp.sin(angle)
    pattern = "tf,f...->t..."
    time_real = jnp.einsum(pattern, cos_table, spectra[0], precision=HIGHEST) - jnp.einsum(
        pattern, sin_table, spectra[1], precision=HIGHEST
    )
    time_imag = jnp.einsum(pattern, sin_table, spectra[0], precision=HIGHEST) + jnp.einsum(
        pattern, cos_table, spectra[1], precision=HIGHEST
    )
    magnitude = jnp.sqrt(time_real * time_real + time_imag * time_imag)
    factor = (
        jnp.maximum(magnitude - shrink_level, 0.0) / jnp.maximum(magnitude, shrink_level) * keep
    )
    kept_real = factor * time_real
    kept_imag = factor * time_imag
    back_real = (
        jnp.einsum(pattern, cos_table, kept_real, precision=HIGHEST)
        + jnp.einsum(pattern, sin_table, kept_imag, precision=HIGHEST)
    ) / n_freq
    back_imag = (
        jnp.einsum(pattern, cos_table, kept_imag, precision=HIGHEST)
        - jnp.einsum(pattern, sin_table, kept_real, precision=HIGHEST)
    ) / n_freq
    return jnp.stack([back_real, back_imag])


def on_device(green_freq, data_matrix, shot_panels, wavelet, sources, support, threshold):
    data_pair = (data_matrix[0], data_matrix[1])
    picked = jnp.take(green_freq, sources, axis=3)
    wave_real = wavelet[0][:, None, None]
    wave_imag = wavelet[1][:, None, None]
    rows_here = green_freq.shape[2]
    shard_piece = lax.all_gather(picked, "rcv", axis=2, tiled=True)
    block_real = data_matrix[0]
    block_imag = data_matrix[1]
    real_part, imag_part = complex_product(
        (block_real, block_imag), (shard_piece[0], shard_piece[1]), "frk,fkc->frc"
    )
    multiple = jnp.stack([real_part, imag_part])
    resid_real = shot_panels[0] - (wave_real * picked[0] - wave_imag * picked[1] - multiple[0])
    resid_imag = shot_panels[1] - (wave_real * picked[1] + wave_imag * picked[0] - multiple[1])
    residual = jnp.stack([resid_real, resid_imag])
    local_real = wave_real * resid_real + wave_imag * resid_imag
    local_imag = wave_real * resid_imag - wave_imag * resid_real
    adj_real, adj_imag = conj_product(data_pair, (resid_real, resid_imag), "frk,frc->kfc")
    summed_terms = -jnp.stack([adj_real, adj_imag], axis=1)
    own_rows = jnp.transpose(jnp.stack([local_real, local_imag]), (2, 0, 1, 3))
    row_offset = lax.axis_index("rcv") * rows_here
    summed_terms = summed_terms + lax.dynamic_update_slice_in_dim(
        jnp.zeros_like(summed_terms), own_rows, row_offset, 0
    )
    summed_all = lax.psum(summed_terms, "rcv")
    mine = lax.dynamic_slice_in_dim(summed_all, row_offset, rows_here, 0)
    direction = jnp.transpose(mine, (1, 2, 0, 3))
    push_real, push_imag = complex_product(
        data_pair, (summed_all[:, 0], summed_all[:, 1]), "frk,kfc->frc"
    )
    pushed = jnp.stack([push_real, push_imag])
    image_real = wave_real * direction[0] - wave_imag * direction[1] - pushed[0]
    image_imag = wave_real * direction[1] + wave_imag * direction[0] - pushed[1]
    norm_dir = jnp.sum(direction * direction)
    norm_img = jnp.sum(image_real * image_real + image_imag * image_imag)
    totals = lax.psum((norm_dir, norm_img), ("freq", "rcv"))
    step_size = totals[0] / totals[1]
    updated = green_freq.at[:, :, :, sources].add(step_size * direction)
    keep_all = support.astype(jnp.float32)
    gathered = lax.all_to_all(updated, "freq", split_axis=2, concat_axis=1, tiled=True)
    shrunk = shrink_spectra(gathered, keep_all[:, None, :], threshold[0])
    green_next = lax.all_to_all(shrunk, "freq", split_axis=1, concat_axis=2, tiled=True)
    return (green_next, residual)


def solution(mesh):
    in_specs = (
        P(None, "freq", "rcv", None),
        P(None, "freq", "rcv", None),
        P(None, "freq", "rcv", None),
        P(None, "freq"),
        P(),
        P(),
        P(),
    )
    out_specs = (P(None, "freq", "rcv", None), P(None, "freq", "rcv", None))
    return jax.shard_map(
        on_device, mesh=mesh, in_specs=in_specs, out_specs=out_specs, check_vma=False
    )
```

profile of v0, /device:TPU:0, one launch (start us, length us, event | category | flops | bytes accessed | tf_op | source)
XLA Modules:
  0.0 851.4 jit_solution(611839117997585425)
XLA Ops:
  8.6 19.2 %copy.30 = f32[2,1,576,2304]{2,0,3,1:T(2,128)} copy(f32[2,1,576,2304]{3,2,1,0:T(8,128)} %param.7) | data formatting | bytes 21233664 | tf_op args[0]
  27.8 6.5 gather_fusion
  37.8 91.2 %all-gather.2.cloned.1.call-done = f32[2,1,2304,256]{3,2,1,0:T(8,128)} async-done(((f32[2,1,576,256]{3,2,1,0:T(8,128)}), f32[2,1,2304,256]{3,2,1,0:T(8,128)}) %all-gather.2.cloned.1.call-update) | async-done | bytes 4718608 | tf_op jit(solution)/shard_map/all_gather | solution.py:71
  129.0 7.5 fusion.8
  136.6 9.7 %fusion.101 = f32[576,256]{1,0:T(8,128)S(1)} fusion(f32[256,576]{0,1:T(8,128)S(1)} %fusion.8, f32[2,1,576,2304]{3,2,1,0:T(8,128)} %param.8, f32[2,1,2304,256]{3,2,1,0:T(8,128)} %all-gather.2.cloned.1.call-done, f32[2,1,576,256]{3,2,1,0:T(8,128)} %param.9, f32[2,1,576,256]{3,2,1,0:T(8,128)S(1)} %copy-done.2, f32[]{:T(128)} %bitcast.6, f32[]{:T(128)} %bitcast.3), kind=kOutput, calls=%fused_computation.76 | convolution fusion | flops 4077748224 | bytes 10617856 | tf_op jit(solution)/shard_map/frk,fkc->frc/dot_general | solution.py:16
  146.3 11.9 %fusion.6 = f32[256,2304]{0,1:T(8,128)S(1)} fusion(f32[576,256]{1,0:T(8,128)S(1)} %fusion.101, f32[2,1,576,2304]{3,2,1,0:T(8,128)} %param.8), kind=kOutput, calls=%fused_computation.9 | convolution fusion | flops 4076863488 | bytes 8257536 | tf_op jit(solution)/shard_map/frk,frc->kfc/dot_general | solution.py:25
  162.6 5.7 fusion.98
  168.3 9.6 %fusion.4 = f32[256,2304]{0,1:T(8,128)S(1)} fusion(f32[576,256]{1,0:T(8,128)S(1)} %fusion.98, f32[2,1,576,2304]{3,2,1,0:T(8,128)S(1)} %bitcast.238), kind=kOutput, calls=%fused_computation.7 | convolution fusion | flops 4076863488 | bytes 8257536 | tf_op jit(solution)/shard_map/frk,frc->kfc/dot_general | solution.py:28
  179.3 9.7 %fusion.41 = f32[2304,1,1,256]{3,0,2,1:T(8,128)S(1)} fusion(f32[256,2304]{0,1:T(8,128)S(1)} %fusion.6, f32[576,256]{1,0:T(8,128)S(1)} %fusion.98, f32[2,1,576,2304]{3,2,1,0:T(8,128)S(1)} %bitcast.238), kind=kOutput, calls=%fused_computation.44 | convolution fusion | flops 4077453312 | bytes 10616832 | tf_op jit(solution)/shard_map/frk,frc->kfc/dot_general | solution.py:25
  189.0 9.9 %fusion.38 = f32[2304,1,1,256]{3,0,2,1:T(8,128)S(1)} fusion(f32[256,2304]{0,1:T(8,128)S(1)} %fusion.4, f32[576,256]{1,0:T(8,128)S(1)} %fusion.101, f32[2,1,576,2304]{3,2,1,0:T(8,128)S(1)} %bitcast.238), kind=kOutput, calls=%fused_computation.43 | convolution fusion | flops 4077453312 | bytes 10616832 | tf_op jit(solution)/shard_map/frk,frc->kfc/dot_general | solution.py:28
  203.8 170.5 %all-reduce.3.cloned.1.call-done = f32[2304,2,1,256]{3,0,2,1:T(8,128)} async-done(((f32[2304,2,1,256]{3,0,2,1:T(8,128)}), f32[2304,2,1,256]{3,0,2,1:T(8,128)}) %all-reduce.3.cloned.1.call-update) | async-done | bytes 4718608 | tf_op jit(solution)/shard_map/psum | solution.py:90
  376.7 7.8 fusion
  384.5 7.0 fusion.2
  391.5 5.6 fusion.83
  397.2 6.3 fusion.109
  403.5 39.4 %all-reduce = (f32[]{:T(128)}, f32[]{:T(128)}) all-reduce(f32[]{:T(128)} %get-tuple-element.8, f32[]{:T(128)} %fusion.109), channel_id=1, replica_groups=mesh['freq'=8,'rcv'=4] {'freq','rcv'}, use_global_device_ids=true, to_apply=%region_2.3 | all-reduce | flops 2 | bytes 16 | tf_op jit(solution)/shard_map/psum | solution.py:101
  449.2 31.0 %scatter_fusion = f32[2,576,2304]{1,0,2:T(2,128)} fusion(f32[2,576,2304]{1,0,2:T(2,128)} %bitcast.242, s32[256]{0:T(256)S(1)} %compare_select_fusion, f32[256,2,576]{2,1,0:T(2,128)S(1)} %copy.36), kind=kCustom, calls=%fused_computation.1 | custom fusion | flops 294912 | bytes 3539968 | tf_op jit(solution)/shard_map/scatter-add | solution.py:103
  480.3 21.2 %copy.37 = f32[2,1,576,2304]{3,0,1,2:T(2,128)} copy(f32[2,1,576,2304]{2,0,3,1:T(2,128)} %bitcast.243) | data formatting | bytes 21233664 | tf_op jit(solution)/shard_map/scatter-add | solution.py:103
  501.5 5.3 all-to-all-start
  507.5 117.2 %all-to-all-done = f32[2,1,576,2304]{3,0,1,2:T(2,128)} async-done(((f32[2,1,576,2304]{3,0,1,2:T(2,128)}), f32[2,1,576,2304]{3,0,1,2:T(2,128)}, u32[]{:S(2)}, u32[]{:S(2)}) %all-to-all-start) | async-done | bytes 10616864 | tf_op jit(solution)/shard_map/all_to_all | solution.py:105
  624.7 12.6 %fusion.174 = (f32[1,1,576,2304]{3,0,1,2:T(1,128)S(1)}, f32[1,1,576,2304]{3,0,1,2:T(1,128)S(1)}) fusion(f32[2,1,576,2304]{3,0,1,2:T(2,128)} %all-to-all-done), kind=kLoop, calls=%fused_computation.145 | loop fusion | bytes 21233664 | tf_op jit(solution)/shard_map/slice | solution.py:43
  637.7 7.0 fusion.30
  644.7 7.0 fusion.28
  652.1 7.1 convolution_subtract_fusion
  659.2 7.4 convolution_add_fusion
  666.6 7.6 fusion.121
  674.3 8.0 fusion.119
  682.3 8.8 %multiply_bitcast_fusion.1 = f32[1,8,72,2304]{3,1,2,0:T(8,128)} fusion(f32[8,72,2304]{2,0,1:T(8,128)S(1)} %fusion.121, f32[8,72,2304]{2,0,1:T(8,128)S(1)} %convolution_add_fusion, f32[8,72,2304]{2,0,1:T(8,128)S(1)} %convolution_subtract_fusion, f32[8,2304]{1,0:T(8,128)S(1)} %convert_element_type.21, f32[]{:T(128)} %bitcast.234), kind=kOutput, calls=%fused_computation.28 | convolution fusion | flops 142001024 | bytes 21307396 | tf_op jit(solution)/shard_map/tf,f...->t.../dot_general | solution.py:56
  691.1 9.0 %multiply_bitcast_fusion = f32[1,8,72,2304]{3,1,2,0:T(8,128)} fusion(f32[8,72,2304]{2,0,1:T(8,128)S(1)} %fusion.119, f32[8,72,2304]{2,0,1:T(8,128)S(1)} %convolution_subtract_fusion, f32[8,72,2304]{2,0,1:T(8,128)S(1)} %convolution_add_fusion, f32[8,2304]{1,0:T(8,128)S(1)} %convert_element_type.21, f32[]{:T(128)} %bitcast.235), kind=kOutput, calls=%fused_computation.27 | convolution fusion | flops 142001024 | bytes 21307396 | tf_op jit(solution)/shard_map/tf,f...->t.../dot_general | solution.py:60
  704.9 7.4 copy.44
  718.5 116.8 %all-to-all-done.1 = f32[2,8,72,2304]{3,2,0,1:T(8,128)} async-done(((f32[2,8,72,2304]{3,2,0,1:T(8,128)}), f32[2,8,72,2304]{3,2,0,1:T(8,128)}, u32[]{:S(2)}, u32[]{:S(2)}) %all-to-all-start.1) | async-done | bytes 10616864 | tf_op jit(solution)/shard_map/all_to_all | solution.py:107
  835.3 9.0 %copy.45 = f32[2,8,72,2304]{3,2,1,0:T(8,128)} copy(f32[2,8,72,2304]{3,2,0,1:T(8,128)} %all-to-all-done.1) | data formatting | bytes 21233664 | tf_op jit(solution)/shard_map/all_to_all | solution.py:107
  (54 shorter events, 34.6 us)
Async XLA Ops:
  7.2 121.9 %all-gather.2.cloned.1.call-start = ((), (), s32[]{:S(2)}) async-start(), calls=%async_computation.2 | async-start | bytes 5898240 | tf_op jit(solution)/shard_map/all_gather | solution.py:71
  27.8 9.3 %copy-start.5 = (f32[2,1]{0,1:T(1,128)S(1)}, f32[2,1]{0,1:T(1,128)}, u32[]{:S(2)}) copy-start(f32[2,1]{0,1:T(1,128)} %param.10) | copy-start | bytes 28
  36.7 99.8 %copy-start.2 = (f32[2,1,576,256]{3,2,1,0:T(8,128)S(1)}, f32[2,1,576,256]{3,2,1,0:T(8,128)}, u32[]{:S(2)}) copy-start(f32[2,1,576,256]{3,2,1,0:T(8,128)} %bitcast_select_fusion) | copy-start | bytes 3538948
  36.8 337.6 %all-reduce.3.cloned.1.call-start = ((), (), s32[]{:S(2)}) async-start(), calls=%async_computation.3 | async-start | bytes 9437184 | tf_op jit(solution)/shard_map/psum | solution.py:90
  129.0 29.2 %slice-start = ((s8[10616832]{0:T(1024)(128)(4,1)}), s8[4194304]{0:T(1024)(128)(4,1)S(1)}, s32[]{:S(2)}) async-start(s8[10616832]{0:T(1024)(128)(4,1)} %bitcast.237), calls=%async_computation.4 | async-start | bytes 8388608
  129.0 29.2 %slice-start.6 = ((s8[4718592]{0:T(1024)(128)(4,1)}), s8[4194304]{0:T(1024)(128)(4,1)S(1)}, s32[]{:S(2)}) async-start(s8[4718592]{0:T(1024)(128)(4,1)} %bitcast.248), calls=%async_computation.10 | async-start | bytes 8388608
  136.5 21.7 %slice-start.1 = ((s8[10616832]{0:T(1024)(128)(4,1)}), s8[4194304]{0:T(1024)(128)(4,1)S(1)}, s32[]{:S(2)}) async-start(s8[10616832]{0:T(1024)(128)(4,1)} %bitcast.237), calls=%async_computation.5 | async-start | bytes 8388608
  136.5 21.7 %slice-start.2 = ((s8[10616832]{0:T(1024)(128)(4,1)}), s8[2228224]{0:T(1024)(128)(4,1)S(1)}, s32[]{:S(2)}) async-start(s8[10616832]{0:T(1024)(128)(4,1)} %bitcast.237), calls=%async_computation.6 | async-start | bytes 4456448
  136.5 21.7 %slice-start.7 = ((s8[4718592]{0:T(1024)(128)(4,1)}), s8[524288]{0:T(1024)(128)(4,1)S(1)}, s32[]{:S(2)}) async-start(s8[4718592]{0:T(1024)(128)(4,1)} %bitcast.248), calls=%async_computation.11 | async-start | bytes 1048576
  158.2 4.4 copy-start.3
  203.8 187.7 %slice-start.3 = ((s8[10616832]{0:T(1024)(128)(4,1)}), s8[2228224]{0:T(1024)(128)(4,1)S(1)}, s32[]{:S(2)}) async-start(s8[10616832]{0:T(1024)(128)(4,1)} %bitcast.239), calls=%async_computation.7 | async-start | bytes 4456448
  374.4 10.2 %copy-start = (f32[2304,2,1,256]{3,0,2,1:T(8,128)S(1)}, f32[2304,2,1,256]{3,0,2,1:T(8,128)}, u32[]{:S(2)}) copy-start(f32[2304,2,1,256]{3,0,2,1:T(8,128)} %all-reduce.3.cloned.1.call-done) | copy-start | bytes 14155780
  376.7 20.5 %copy-start.1 = (f32[2,1,576,256]{3,2,1,0:T(8,128)}, f32[2,1,576,256]{3,2,1,0:T(8,128)S(1)}, u32[]{:S(2)}) copy-start(f32[2,1,576,256]{3,2,1,0:T(8,128)S(1)} %get-tuple-element.9) | copy-start | bytes 3538948
  376.7 14.8 %slice-start.4 = ((s8[10616832]{0:T(1024)(128)(4,1)}), s8[4194304]{0:T(1024)(128)(4,1)S(1)}, s32[]{:S(2)}) async-start(s8[10616832]{0:T(1024)(128)(4,1)} %bitcast.239), calls=%async_computation.8 | async-start | bytes 8388608
  384.5 7.0 slice-start.5
  501.5 5.3 copy-start.4
  501.5 123.2 %all-to-all-start = ((f32[2,1,576,2304]{3,0,1,2:T(2,128)}), f32[2,1,576,2304]{3,0,1,2:T(2,128)}, u32[]{:S(2)}, u32[]{:S(2)}) async-start(f32[2,1,576,2304]{3,0,1,2:T(2,128)} %copy.37), calls=%async_computation | async-start | bytes 21233664 | tf_op jit(solution)/shard_map/all_to_all | solution.py:105
  712.2 123.1 %all-to-all-start.1 = ((f32[2,8,72,2304]{3,2,0,1:T(8,128)}), f32[2,8,72,2304]{3,2,0,1:T(8,128)}, u32[]{:S(2)}, u32[]{:S(2)}) async-start(f32[2,8,72,2304]{3,2,0,1:T(8,128)} %copy.44), calls=%async_computation.1 | async-start | bytes 21233664 | tf_op jit(solution)/shard_map/all_to_all | solution.py:107
Sparse Core Ops, SparseCore 0:
  36.9 92.0 all-gather.1
  203.9 170.3 all-reduce.2
where the time goes:
time: 856 us; the launch traced here: 851 us
  waiting for transfers between devices  496 us (58%)
  matrix products  157 us (18%)
  local copies, waits for them, and re-layouts  81.3 us (9%)
  other arithmetic  50.4 us (6%)
  blocking collectives  39.4 us (5%)
  between operations  16.6 us (2%)
  starting transfers between devices  10.8 us (1%)
    psum x1, waiting for transfers between devices, on_device(): summed_all = lax.psum(summed_terms, 'rcv')  171 us
    all_to_all x1, waiting for transfers between devices, on_device(): lax.all_to_all(updated, 'freq', split_axis=2, concat_axis=1, tiled=True)  117 us
    all_to_all x1, waiting for transfers between devices, on_device(): lax.all_to_all(shrunk, 'freq', split_axis=1, concat_axis=2, tiled=True)  117 us
    all_gather x1, waiting for transfers between devices, on_device(): shard_piece = lax.all_gather(picked, 'rcv', axis=2, tiled=True)  91.2 us
    psum x1, blocking collectives, on_device(): totals = lax.psum((norm_dir, norm_img), ('freq', 'rcv'))  39.4 us
    scatter-add x1, other arithmetic, on_device(): updated = green_freq.at[:, :, :, sources].add(step_size * direction)  31 us
    scatter-add x1, local copies, waits for them, and re-layouts, on_device(): updated = green_freq.at[:, :, :, sources].add(step_size * direction)  21.2 us
    unnamed x31, local copies, waits for them, and re-layouts  20 us
  transfers between devices with their start and end apart: 4, of which 4 were waited for; matrix products, arithmetic and copies ran while one was open for 0% of the time, Pallas kernels for 0%

commit v1 on v0

--- a/solution.py
+++ b/solution.py
@@ -87,7 +87,7 @@
     summed_terms = summed_terms + lax.dynamic_update_slice_in_dim(
         jnp.zeros_like(summed_terms), own_rows, row_offset, 0
     )
-    summed_all = lax.psum(summed_terms, "rcv")
+    summed_all = jnp.sum(lax.all_gather(summed_terms, "rcv"), axis=0)
     mine = lax.dynamic_slice_in_dim(summed_all, row_offset, rows_here, 0)
     direction = jnp.transpose(mine, (1, 2, 0, 3))
     push_real, push_imag = complex_product(

time: 856 us -> 1020 us (1.19)
  waiting for transfers between devices: 496 us -> 647 us
    all_gather x0 -> x1, waiting for transfers between devices: none -> 321 us  [on_device(): summed_all = jnp.sum(lax.all_gather(summed_terms, 'rcv'), axis=0)]
    psum x1 -> x0, waiting for transfers between devices: 171 us -> none  [on_device(): summed_all = lax.psum(summed_terms, 'rcv')]
    reduce_sum x0 -> x1, other arithmetic: none -> 10.5 us  [on_device(): summed_all = jnp.sum(lax.all_gather(summed_terms, 'rcv'), axis=0)]
where the time goes in v1:
time: 1020 us; the launch traced here: 1010 us
  waiting for transfers between devices  647 us (63%)
  matrix products  160 us (16%)
  local copies, waits for them, and re-layouts  80.6 us (8%)
  other arithmetic  58.3 us (6%)
  blocking collectives  39.3 us (4%)
  between operations  16.7 us (2%)
  starting transfers between devices  10.7 us (1%)
    all_gather x1, waiting for transfers between devices, on_device(): summed_all = jnp.sum(lax.all_gather(summed_terms, 'rcv'), axis=0)  321 us
    all_to_all x1, waiting for transfers between devices, on_device(): lax.all_to_all(updated, 'freq', split_axis=2, concat_axis=1, tiled=True)  117 us
    all_to_all x1, waiting for transfers between devices, on_device(): lax.all_to_all(shrunk, 'freq', split_axis=1, concat_axis=2, tiled=True)  117 us
    all_gather x1, waiting for transfers between devices, on_device(): shard_piece = lax.all_gather(picked, 'rcv', axis=2, tiled=True)  91.4 us
    psum x1, blocking collectives, on_device(): totals = lax.psum((norm_dir, norm_img), ('freq', 'rcv'))  39.3 us
    scatter-add x1, other arithmetic, on_device(): updated = green_freq.at[:, :, :, sources].add(step_size * direction)  31 us
    scatter-add x1, local copies, waits for them, and re-layouts, on_device(): updated = green_freq.at[:, :, :, sources].add(step_size * direction)  21.2 us
  transfers between devices with their start and end apart: 4, of which 4 were waited for; matrix products, arithmetic and copies ran while one was open for 0% of the time, Pallas kernels for 0%

profile of v1, /device:TPU:0, one launch (start us, length us, event | category | flops | bytes accessed | tf_op | source)
XLA Modules:
  0.0 1011.8 jit_solution(6764799808991410115)
XLA Ops:
  8.6 19.2 %copy.32 = f32[2,1,576,2304]{2,0,3,1:T(2,128)} copy(f32[2,1,576,2304]{3,2,1,0:T(8,128)} %param.7) | data formatting | bytes 21233664 | tf_op args[0]
  27.8 6.5 gather_fusion
  37.6 91.4 %all-gather.3.cloned.1.call-done = f32[2,1,2304,256]{3,2,1,0:T(8,128)} async-done(((f32[2,1,576,256]{3,2,1,0:T(8,128)}), f32[2,1,2304,256]{3,2,1,0:T(8,128)}) %all-gather.3.cloned.1.call-update) | async-done | bytes 4718608 | tf_op jit(solution)/shard_map/all_gather | solution.py:71
  129.0 7.5 fusion.8
  136.5 9.4 fusion.95
  145.9 11.6 %fusion.6 = f32[256,2304]{0,1:T(8,128)S(1)} fusion(f32[576,256]{1,0:T(8,128)S(1)} %fusion.95, f32[2,1,576,2304]{3,2,1,0:T(8,128)} %param.8), kind=kOutput, calls=%fused_computation.9 | convolution fusion | flops 4076863488 | bytes 8257536 | tf_op jit(solution)/shard_map/frk,frc->kfc/dot_general | solution.py:25
  162.0 5.7 fusion.92
  167.7 10.4 %fusion.4 = f32[256,2304]{0,1:T(8,128)S(1)} fusion(f32[576,256]{1,0:T(8,128)S(1)} %fusion.92, f32[2,1,576,2304]{3,2,1,0:T(8,128)S(1)} %bitcast.243), kind=kOutput, calls=%fused_computation.7 | convolution fusion | flops 4076863488 | bytes 8257536 | tf_op jit(solution)/shard_map/frk,frc->kfc/dot_general | solution.py:28
  179.6 9.7 fusion.32
  189.3 9.8 fusion.35
  202.7 321.1 %all-gather.5.cloned.1.call-done = f32[4,2304,2,1,256]{4,1,3,2,0:T(8,128)} async-done(((f32[1,2304,2,1,256]{4,1,3,2,0:T(8,128)}), f32[4,2304,2,1,256]{4,1,3,2,0:T(8,128)}) %all-gather.5.cloned.1.call-update) | async-done | bytes 18874384 | tf_op jit(solution)/shard_map/all_gather | solution.py:90
  523.8 10.5 %reduce_sum.29 = f32[2304,2,256]{2,0,1:T(8,128)} reduce(f32[4,2304,2,1,256]{4,1,3,2,0:T(8,128)} %all-gather.5.cloned.1.call-done, f32[]{:T(128)} %constant.49.clone.1), dimensions={0,3}, to_apply=%region_0.1 | reduce | flops 3538944 | bytes 23592964 | tf_op jit(solution)/shard_map/reduce_sum | solution.py:90
  536.6 7.5 fusion
  544.1 6.8 fusion.2
  551.0 8.5 fusion.77
  559.5 6.3 fusion.106
  565.8 39.3 %all-reduce = (f32[]{:T(128)}, f32[]{:T(128)}) all-reduce(f32[]{:T(128)} %get-tuple-element.8, f32[]{:T(128)} %fusion.106), channel_id=1, replica_groups=mesh['freq'=8,'rcv'=4] {'freq','rcv'}, use_global_device_ids=true, to_apply=%region_2.3 | all-reduce | flops 2 | bytes 16 | tf_op jit(solution)/shard_map/psum | solution.py:101
  610.2 31.0 %scatter_fusion = f32[2,576,2304]{1,0,2:T(2,128)} fusion(f32[2,576,2304]{1,0,2:T(2,128)} %bitcast.247, s32[256]{0:T(256)S(1)} %compare_select_fusion, f32[256,2,576]{2,1,0:T(2,128)S(1)} %copy.39), kind=kCustom, calls=%fused_computation.1 | custom fusion | flops 294912 | bytes 3539968 | tf_op jit(solution)/shard_map/scatter-add | solution.py:103
  641.2 21.2 %copy.40 = f32[2,1,576,2304]{3,0,1,2:T(2,128)} copy(f32[2,1,576,2304]{2,0,3,1:T(2,128)} %bitcast.248) | data formatting | bytes 21233664 | tf_op jit(solution)/shard_map/scatter-add | solution.py:103
  668.4 117.2 %all-to-all-done = f32[2,1,576,2304]{3,0,1,2:T(2,128)} async-done(((f32[2,1,576,2304]{3,0,1,2:T(2,128)}), f32[2,1,576,2304]{3,0,1,2:T(2,128)}, u32[]{:S(2)}, u32[]{:S(2)}) %all-to-all-start) | async-done | bytes 10616864 | tf_op jit(solution)/shard_map/all_to_all | solution.py:105
  785.6 12.0 %fusion.171 = (f32[1,1,576,2304]{3,0,1,2:T(1,128)S(1)}, f32[1,1,576,2304]{3,0,1,2:T(1,128)S(1)}) fusion(f32[2,1,576,2304]{3,0,1,2:T(2,128)} %all-to-all-done), kind=kLoop, calls=%fused_computation.148 | loop fusion | bytes 21233664 | tf_op jit(solution)/shard_map/slice | solution.py:43
  798.0 7.0 fusion.30
  805.0 7.1 fusion.28
  812.4 7.1 convolution_subtract_fusion
  819.6 7.6 convolution_add_fusion
  827.2 7.6 fusion.118
  834.8 7.8 fusion.116
  842.6 8.9 multiply_bitcast_fusion.1
  851.4 9.0 multiply_bitcast_fusion
  865.2 7.4 copy.47
  878.9 116.8 %all-to-all-done.1 = f32[2,8,72,2304]{3,2,0,1:T(8,128)} async-done(((f32[2,8,72,2304]{3,2,0,1:T(8,128)}), f32[2,8,72,2304]{3,2,0,1:T(8,128)}, u32[]{:S(2)}, u32[]{:S(2)}) %all-to-all-start.1) | async-done | bytes 10616864 | tf_op jit(solution)/shard_map/all_to_all | solution.py:107
  995.7 9.0 copy.48
  (53 shorter events, 37.2 us)
Async XLA Ops:
  7.2 121.8 %all-gather.3.cloned.1.call-start = ((), (), s32[]{:S(2)}) async-start(), calls=%async_computation.2 | async-start | bytes 5898240 | tf_op jit(solution)/shard_map/all_gather | solution.py:71
  27.8 9.2 copy-start.4
  36.7 99.8 %copy-start.1 = (f32[2,1,576,256]{3,2,1,0:T(8,128)S(1)}, f32[2,1,576,256]{3,2,1,0:T(8,128)}, u32[]{:S(2)}) copy-start(f32[2,1,576,256]{3,2,1,0:T(8,128)} %bitcast_select_fusion) | copy-start | bytes 3538948
  36.7 99.8 %copy-start.2 = (f32[2,1,576,256]{3,2,1,0:T(8,128)S(1)}, f32[2,1,576,256]{3,2,1,0:T(8,128)}, u32[]{:S(2)}) copy-start(f32[2,1,576,256]{3,2,1,0:T(8,128)} %param.9) | copy-start | bytes 3538948
  36.7 487.1 %all-gather.5.cloned.1.call-start = ((), (), s32[]{:S(2)}) async-start(), calls=%async_computation.3 | async-start | bytes 23592960 | tf_op jit(solution)/shard_map/all_gather | solution.py:90
  129.0 28.5 %slice-start = ((s8[10616832]{0:T(1024)(128)(4,1)}), s8[4194304]{0:T(1024)(128)(4,1)S(1)}, s32[]{:S(2)}) async-start(s8[10616832]{0:T(1024)(128)(4,1)} %bitcast.242), calls=%async_computation.4 | async-start | bytes 8388608
  129.0 28.5 %slice-start.6 = ((s8[4718592]{0:T(1024)(128)(4,1)}), s8[4194304]{0:T(1024)(128)(4,1)S(1)}, s32[]{:S(2)}) async-start(s8[4718592]{0:T(1024)(128)(4,1)} %bitcast.261), calls=%async_computation.10 | async-start | bytes 8388608
  136.5 21.0 %slice-start.1 = ((s8[10616832]{0:T(1024)(128)(4,1)}), s8[4194304]{0:T(1024)(128)(4,1)S(1)}, s32[]{:S(2)}) async-start(s8[10616832]{0:T(1024)(128)(4,1)} %bitcast.242), calls=%async_computation.5 | async-start | bytes 8388608
  136.5 21.0 %slice-start.2 = ((s8[10616832]{0:T(1024)(128)(4,1)}), s8[2228224]{0:T(1024)(128)(4,1)S(1)}, s32[]{:S(2)}) async-start(s8[10616832]{0:T(1024)(128)(4,1)} %bitcast.242), calls=%async_computation.6 | async-start | bytes 4456448
  136.5 21.0 %slice-start.7 = ((s8[4718592]{0:T(1024)(128)(4,1)}), s8[524288]{0:T(1024)(128)(4,1)S(1)}, s32[]{:S(2)}) async-start(s8[4718592]{0:T(1024)(128)(4,1)} %bitcast.261), calls=%async_computation.11 | async-start | bytes 1048576
  534.3 9.8 copy-start
  536.6 22.9 %slice-start.3 = ((s8[10616832]{0:T(1024)(128)(4,1)}), s8[4194304]{0:T(1024)(128)(4,1)S(1)}, s32[]{:S(2)}) async-start(s8[10616832]{0:T(1024)(128)(4,1)} %bitcast.244), calls=%async_computation.7 | async-start | bytes 8388608
  544.1 15.4 %slice-start.4 = ((s8[10616832]{0:T(1024)(128)(4,1)}), s8[4194304]{0:T(1024)(128)(4,1)S(1)}, s32[]{:S(2)}) async-start(s8[10616832]{0:T(1024)(128)(4,1)} %bitcast.244), calls=%async_computation.8 | async-start | bytes 8388608
  550.9 8.6 slice-start.5
  662.4 5.3 copy-start.3
  662.4 123.2 %all-to-all-start = ((f32[2,1,576,2304]{3,0,1,2:T(2,128)}), f32[2,1,576,2304]{3,0,1,2:T(2,128)}, u32[]{:S(2)}, u32[]{:S(2)}) async-start(f32[2,1,576,2304]{3,0,1,2:T(2,128)} %copy.40), calls=%async_computation | async-start | bytes 21233664 | tf_op jit(solution)/shard_map/all_to_all | solution.py:105
  872.6 123.1 %all-to-all-start.1 = ((f32[2,8,72,2304]{3,2,0,1:T(8,128)}), f32[2,8,72,2304]{3,2,0,1:T(8,128)}, u32[]{:S(2)}, u32[]{:S(2)}) async-start(f32[2,8,72,2304]{3,2,0,1:T(8,128)} %copy.47), calls=%async_computation.1 | async-start | bytes 21233664 | tf_op jit(solution)/shard_map/all_to_all | solution.py:107
Sparse Core Ops, SparseCore 0:
  36.8 92.0 all-gather.2
  202.8 320.9 all-gather.4
